TPU v7x, 32 devices: a whole 2x2x4 slice. The times are simulated.
32 devices in a mesh: dp: 8 (over z, x), mp: 4 (over y, core).
Axes of the slice: x: 2, y: 2, z: 4, core: 2. Of those that a mesh axis runs over, the one named last changes fastest.
Arguments:
- activations: bfloat16 [4096, 3072], P('dp', 'mp'), may hold values from -6 to 6
- out_grads: bfloat16 [4096, 6144], P('dp', 'mp'), may hold values from -0.25 to 0.25
- error: bfloat16 [8, 3072, 6144], P('dp', 'mp'), may hold values from -8 to 8
- sketch: bfloat16 [6144, 64], replicated, may hold values from -0.078125 to 0.078125
- momentum: float32 [3072, 6144], P('mp', 'dp'), may hold values from -6 to 6
Outputs:
- error_new: bfloat16 [8, 3072, 6144], P('dp', 'mp')
- momentum_new: float32 [3072, 6144], P('mp', 'dp')
- next_sketch: bfloat16 [6144, 64], replicated
All inputs are finite; a program needn't handle non-finite values.
Results may differ from a plain program's by a relative error of at most 0.0057.
Values may be sent and summed in bfloat16 or wider, within the bound.
A program may use at most 64 MiB of HBM per device.

v0:
```python
import jax
import jax.numpy as jnp
from jax import lax
from jax.sharding import PartitionSpec as P

beta_decay = 0.9


def update_momentum(momentum, basis_rows, sketch_block):
    product = lax.dot_general(
        basis_rows, sketch_block, (((1,), (1,)), ((), ())), preferred_element_type=jnp.float32
    )
    return beta_decay * momentum + product


def local(activations, out_grads, error, sketch, momentum):
    own_error = error[0]
    product = lax.dot_general(
        activations,
        lax.all_gather(out_grads, "mp", axis=1, tiled=True),
        (((0,), (0,)), ((), ())),
        preferred_element_type=jnp.float32,
    )
    accumulated = (product + own_error.astype(jnp.float32)).astype(jnp.bfloat16)
    local_left = jnp.dot(accumulated, sketch, preferred_element_type=jnp.float32)
    left_sketch = lax.psum(local_left, "dp")
    gram_local = jnp.dot(
        left_sketch.T,
        left_sketch,
        precision=lax.Precision.HIGHEST,
        preferred_element_type=jnp.float32,
    )
    gram_matrix = lax.psum(gram_local, "mp")
    factor = jnp.linalg.cholesky(gram_matrix)
    basis_rows = jax.scipy.linalg.solve_triangular(factor, left_sketch.T, lower=True).T.astype(
        jnp.bfloat16
    )
    block_width = momentum.shape[1]
    local_right = lax.dot_general(
        accumulated, basis_rows, (((0,), (0,)), ((), ())), preferred_element_type=jnp.float32
    )
    right_sketch = lax.psum(local_right, ("dp", "mp"))
    next_sketch = right_sketch.astype(jnp.bfloat16)
    sketch_part = lax.dynamic_slice_in_dim(
        next_sketch, lax.axis_index("dp") * block_width, block_width, 0
    )
    momentum_new = update_momentum(momentum, basis_rows, sketch_part)
    decoded = lax.dot_general(
        basis_rows, next_sketch, (((1,), (1,)), ((), ())), preferred_element_type=jnp.float32
    )
    error_new = (accumulated.astype(jnp.float32) - decoded / lax.axis_size("dp")).astype(
        jnp.bfloat16
    )
    return (error_new[None], momentum_new, next_sketch)


def solution(mesh):
    in_specs = (P("dp", "mp"), P("dp", "mp"), P("dp", "mp", None), P(), P("mp", "dp"))
    out_specs = (P("dp", "mp", None), P("mp", "dp"), P())
    return jax.shard_map(local, mesh=mesh, in_specs=in_specs, out_specs=out_specs, check_vma=False)
```

profile of v0, /device:TPU:0, one launch (start us, length us, event | category | flops | bytes accessed | tf_op | source)
XLA Modules:
  0.0 249.4 jit_solution(14047941913646381180)
XLA Ops:
  7.2 0.0 copy-start
  7.2 0.0 all-gather.2.cloned.1.call-start
  7.2 0.7 all-gather.2.cloned.1.call-update
  7.9 0.0 copy-start.4
  7.9 0.0 all-reduce.3.cloned.1.call-start
  8.0 50.7 %all-gather.2.cloned.1.call-done = bf16[512,6144]{1,0:T(8,128)(2,1)} async-done(((bf16[512,1536]{1,0:T(8,128)(2,1)}), bf16[512,6144]{1,0:T(8,128)(2,1)}) %all-gather.2.cloned.1.call-update) | async-done | bytes 6291472 | tf_op jit(solution)/shard_map/all_gather | solution.py:20
  58.7 0.0 copy-done
  58.7 9.6 %fusion = bf16[768,6144]{1,0:T(8,128)(2,1)S(1)} fusion(bf16[1,768,6144]{2,1,0:T(8,128)(2,1)} %param.7, bf16[512,768]{1,0:T(8,128)(2,1)S(1)} %copy-done, bf16[512,6144]{1,0:T(8,128)(2,1)} %all-gather.2.cloned.1.call-done), kind=kOutput, calls=%fused_computation.1 | convolution fusion | flops 4845993984 | bytes 25952256 | tf_op jit(solution)/shard_map/dot_general | solution.py:18
  68.3 0.0 copy-start.1
  68.3 3.7 %copy-done.1 = bf16[768,6144]{1,0:T(8,128)(2,1)} copy-done((bf16[768,6144]{1,0:T(8,128)(2,1)}, bf16[768,6144]{1,0:T(8,128)(2,1)S(1)}, u32[]{:S(2)}) %copy-start.1) | copy-done | bytes 9437208
  72.1 0.0 copy-done.4
  72.1 3.7 %fusion.7 = f32[768,64]{0,1:T(8,128)} fusion(bf16[768,6144]{1,0:T(8,128)(2,1)S(1)} %fusion, bf16[6144,64]{0,1:T(8,128)(2,1)S(1)} %copy-done.4), kind=kOutput, calls=%fused_computation.17 | convolution fusion | flops 603979776 | bytes 10420224 | tf_op jit(solution)/shard_map/dot_general | solution.py:25
  75.7 0.0 all-reduce.3.cloned.1.call-update
  75.8 70.8 %all-reduce.3.cloned.1.call-done = f32[768,64]{0,1:T(8,128)} async-done(((f32[768,64]{0,1:T(8,128)}), f32[768,64]{0,1:T(8,128)}) %all-reduce.3.cloned.1.call-update) | async-done | bytes 196624 | tf_op jit(solution)/shard_map/psum | solution.py:26
  146.6 1.3 fusion.8
  147.9 10.3 %psum.22 = f32[64,64]{0,1:T(8,128)S(1)} all-reduce(f32[64,64]{0,1:T(8,128)S(1)} %fusion.8), channel_id=1, replica_groups=mesh['dp'=8,'mp'=4] {'mp'}, use_global_device_ids=true, to_apply=%region_1.0 | all-reduce | flops 4096 | bytes 32768 | tf_op jit(solution)/shard_map/psum | solution.py:33
  158.2 0.1 copy.9
  158.3 5.8 %cholesky.16 = f32[64,64]{1,0:T(8,128)S(1)} custom-call(f32[64,64]{1,0:T(8,128)S(1)} %fusion.5), custom_call_target="Cholesky" | custom-call | tf_op jit(solution)/shard_map/jit(cholesky)/cholesky | solution.py:34
  164.2 0.6 compare_reduce_fusion
  164.8 0.7 fusion.3
  165.5 4.9 %custom-call.7 = f32[1,64,64]{1,2,0:T(8,128)S(1)} custom-call(f32[1,64,64]{2,1,0:T(8,128)S(1)} %fusion.3), custom_call_target="InvertDiagBlocksLowerTriangular" | custom-call | tf_op jit(solution)/shard_map/jit(_solve_triangular)/triangular_solve | solution.py:35
  170.4 1.3 convolution_convert_fusion
  171.7 5.4 %fusion.9 = f32[6144,64]{0,1:T(8,128)S(1)} fusion(bf16[768,64]{0,1:T(8,128)(2,1)S(1)} %convolution_convert_fusion, bf16[768,6144]{1,0:T(8,128)(2,1)} %copy-done.1), kind=kOutput, calls=%fused_computation.19 | convolution fusion | flops 603979776 | bytes 11108352 | tf_op jit(solution)/shard_map/dot_general | solution.py:39
  177.1 55.7 %all-reduce.4 = bf16[6144,64]{0,1:T(8,128)(2,1)S(1)} all-reduce(f32[6144,64]{0,1:T(8,128)S(1)} %fusion.9), channel_id=1, replica_groups=mesh['dp'=8,'mp'=4] {'dp','mp'}, use_global_device_ids=true, to_apply=%region_4.5 | all-reduce | flops 393216 | bytes 2359296 | tf_op jit(solution)/shard_map/psum | solution.py:42
  232.8 0.0 copy-start.2
  232.8 0.0 copy-start.3
  232.8 7.8 %fusion.1 = bf16[1,768,6144]{2,1,0:T(8,128)(2,1)} fusion(bf16[768,64]{0,1:T(8,128)(2,1)S(1)} %convolution_convert_fusion, bf16[6144,64]{0,1:T(8,128)(2,1)S(1)} %all-reduce.4, bf16[768,6144]{1,0:T(8,128)(2,1)} %copy-done.1), kind=kOutput, calls=%fused_computation.3 | convolution fusion | flops 622854144 | bytes 19759104 | tf_op jit(solution)/shard_map/dot_general | solution.py:48
  240.7 0.0 copy-done.2
  240.7 0.0 copy-done.3
  240.7 1.9 multiply_add_fusion
  (2 shorter events, 0.0 us)
Async XLA Ops:
  7.2 51.5 %copy-start = (bf16[512,768]{1,0:T(8,128)(2,1)S(1)}, bf16[512,768]{1,0:T(8,128)(2,1)}, u32[]{:S(2)}) copy-start(bf16[512,768]{1,0:T(8,128)(2,1)} %param.5) | copy-start | bytes 2359300
  7.2 51.5 %all-gather.2.cloned.1.call-start = ((), (), s32[]{:S(2)}) async-start(), calls=%async_computation | async-start | bytes 7864320 | tf_op jit(solution)/shard_map/all_gather | solution.py:20
  7.9 64.2 %copy-start.4 = (bf16[6144,64]{0,1:T(8,128)(2,1)S(1)}, bf16[6144,64]{0,1:T(8,128)(2,1)}, u32[]{:S(2)}) copy-start(bf16[6144,64]{0,1:T(8,128)(2,1)} %param.8) | copy-start | bytes 2359300
  7.9 138.7 %all-reduce.3.cloned.1.call-start = ((), (), s32[]{:S(2)}) async-start(), calls=%async_computation.1 | async-start | bytes 393216 | tf_op jit(solution)/shard_map/psum | solution.py:26
  68.3 3.7 %copy-start.1 = (bf16[768,6144]{1,0:T(8,128)(2,1)}, bf16[768,6144]{1,0:T(8,128)(2,1)S(1)}, u32[]{:S(2)}) copy-start(bf16[768,6144]{1,0:T(8,128)(2,1)S(1)} %fusion) | copy-start | bytes 28311556
  232.8 7.8 %copy-start.2 = (bf16[6144,64]{0,1:T(8,128)(2,1)}, bf16[6144,64]{0,1:T(8,128)(2,1)S(1)}, u32[]{:S(2)}) copy-start(bf16[6144,64]{0,1:T(8,128)(2,1)S(1)} %all-reduce.4) | copy-start | bytes 2359300
  232.8 7.8 %copy-start.3 = (f32[768,768]{1,0:T(8,128)S(1)}, f32[768,768]{1,0:T(8,128)}, u32[]{:S(2)}) copy-start(f32[768,768]{1,0:T(8,128)} %param.9) | copy-start | bytes 7077892
Sparse Core Ops, SparseCore 0:
  9.5 49.0 all-gather.1
  75.9 70.6 all-reduce.2
where the time goes:
time: 250 us; the launch traced here: 249 us
  waiting for transfers between devices  122 us (49%)
  blocking collectives  66 us (26%)
  matrix products  31.1 us (12%)
  between operations  14.2 us (6%)
  other arithmetic  12.1 us (5%)
  local copies, waits for them, and re-layouts  3.84 us (2%)
    psum x1, waiting for transfers between devices, local(): left_sketch = lax.psum(local_left, 'dp')  70.8 us
    psum x1, blocking collectives, local(): right_sketch = lax.psum(local_right, ('dp', 'mp'))  55.7 us
    all_gather x1, waiting for transfers between devices, local(): lax.all_gather(out_grads, 'mp', axis=1, tiled=True)  50.7 us
    psum x1, blocking collectives, local(): gram_matrix = lax.psum(gram_local, 'mp')  10.3 us
    dot_general x1, matrix products, local(): lax.dot_general(activations, lax.all_gather(out_grads, 'mp', axis=1, tile...  9.64 us
    dot_general x1, matrix products, local(): lax.dot_general(basis_rows, next_sketch, (((1,), (1,)), ((), ())), prefer...  7.81 us
    another operation x3, other arithmetic, local(): factor = jnp.linalg.cholesky(gram_matrix)  6.52 us
    another operation x2, other arithmetic, local(): jax.scipy.linalg.solve_triangular(factor, left_sketch.T, lower=True)  5.55 us
  transfers between devices with their start and end apart: 2, of which 2 were waited for; matrix products, arithmetic and copies ran while one was open for 0% of the time, Pallas kernels for 0%

commit v1 on v0

--- a/solution.py
+++ b/solution.py
@@ -17,7 +17,9 @@
     own_error = error[0]
     product = lax.dot_general(
         activations,
-        lax.all_gather(out_grads, "mp", axis=1, tiled=True),
+        jnp.concatenate(
+            lax.all_to_all(jnp.stack([out_grads] * lax.axis_size("mp")), "mp", 0, 0), axis=1
+        ),
         (((0,), (0,)), ((), ())),
         preferred_element_type=jnp.float32,
     )

time: 250 us -> 277 us (1.11)
  blocking collectives: 66 us -> 141 us
  waiting for transfers between devices: 122 us -> 71.9 us
    all_to_all x0 -> x1, blocking collectives: none -> 74.9 us  [local(): lax.all_to_all(jnp.stack([out_grads] * lax.axis_size('mp')), 'mp', 0, 0)]
    all_gather x1 -> x0, waiting for transfers between devices: 50.7 us -> none  [local(): lax.all_gather(out_grads, 'mp', axis=1, tiled=True)]
    unnamed x10 -> x11, local copies, waits for them, and re-layouts: 3.76 us -> 5.54 us
  transfers between devices with their start and end apart: 2 -> 1, of which waited for: 2 -> 1; matrix products, arithmetic and copies ran while one was open for 0% -> 0% of each run, Pallas kernels for 0% -> 0%
where the time goes in v1:
time: 277 us
  blocking collectives  141 us (51%)
  waiting for transfers between devices  71.9 us (26%)
  matrix products  31.2 us (11%)
  between operations  14.2 us (5%)
  other arithmetic  12.1 us (4%)
  local copies, waits for them, and re-layouts  6.11 us (2%)
    all_to_all x1, blocking collectives, local(): lax.all_to_all(jnp.stack([out_grads] * lax.axis_size('mp')), 'mp', 0, 0)  74.9 us
    psum x1, waiting for transfers between devices, local(): left_sketch = lax.psum(local_left, 'dp')  71.9 us
    psum x1, blocking collectives, local(): right_sketch = lax.psum(local_right, ('dp', 'mp'))  55.9 us
    psum x1, blocking collectives, local(): gram_matrix = lax.psum(gram_local, 'mp')  10.3 us
    dot_general x1, matrix products, local(): lax.dot_general(activations, jnp.concatenate(lax.all_to_all(jnp.stack([ou...  9.81 us
    dot_general x1, matrix products, local(): lax.dot_general(basis_rows, next_sketch, (((1,), (1,)), ((), ())), prefer...  7.82 us
    another operation x3, other arithmetic, local(): factor = jnp.linalg.cholesky(gram_matrix)  6.52 us
    another operation x2, other arithmetic, local(): jax.scipy.linalg.solve_triangular(factor, left_sketch.T, lower=True)  5.55 us
  transfers between devices with their start and end apart: 1, of which 1 were waited for; matrix products, arithmetic and copies ran while one was open for 0% of the time, Pallas kernels for 0%

profile of v1, /device:TPU:0, one launch (start us, length us, event | category | flops | bytes accessed | tf_op | source)
XLA Modules:
  0.0 276.5 jit_solution(12735940451821131783)
XLA Ops:
  7.2 0.0 copy-start
  7.2 0.0 all-reduce.3.cloned.1.call-start
  7.2 1.8 copy.10
  9.0 0.5 stack.2
  9.5 74.9 %all_to_all.5 = bf16[4,512,1536]{1,2,0:T(8,128)(2,1)} all-to-all(bf16[4,512,1536]{1,2,0:T(8,128)(2,1)S(1)} %stack.2), channel_id=1, replica_groups=mesh['dp'=8,'mp'=4] {'mp'}, dimensions={0} | all-to-all | bytes 12582912 | tf_op jit(solution)/shard_map/all_to_all | solution.py:21
  84.4 0.0 copy-done
  84.4 0.0 copy-start.4
  84.4 9.8 %fusion = bf16[768,6144]{1,0:T(8,128)(2,1)S(1)} fusion(bf16[1,768,6144]{2,1,0:T(8,128)(2,1)} %param.7, bf16[512,768]{1,0:T(8,128)(2,1)S(1)} %copy-done, bf16[512,6144]{0,1:T(8,128)(2,1)} %bitcast.29), kind=kOutput, calls=%fused_computation.1 | convolution fusion | flops 4845993984 | bytes 25952256 | tf_op jit(solution)/shard_map/dot_general | solution.py:18
  94.3 0.0 copy-start.1
  94.3 3.7 %copy-done.1 = bf16[768,6144]{1,0:T(8,128)(2,1)} copy-done((bf16[768,6144]{1,0:T(8,128)(2,1)}, bf16[768,6144]{1,0:T(8,128)(2,1)S(1)}, u32[]{:S(2)}) %copy-start.1) | copy-done | bytes 9437208
  98.0 0.0 copy-done.4
  98.0 3.6 %fusion.7 = f32[768,64]{0,1:T(8,128)} fusion(bf16[768,6144]{1,0:T(8,128)(2,1)S(1)} %fusion, bf16[6144,64]{0,1:T(8,128)(2,1)S(1)} %copy-done.4), kind=kOutput, calls=%fused_computation.17 | convolution fusion | flops 603979776 | bytes 10420224 | tf_op jit(solution)/shard_map/dot_general | solution.py:27
  101.7 0.0 all-reduce.3.cloned.1.call-update
  101.7 71.9 %all-reduce.3.cloned.1.call-done = f32[768,64]{0,1:T(8,128)} async-done(((f32[768,64]{0,1:T(8,128)}), f32[768,64]{0,1:T(8,128)}) %all-reduce.3.cloned.1.call-update) | async-done | bytes 196624 | tf_op jit(solution)/shard_map/psum | solution.py:28
  173.5 1.3 fusion.8
  174.9 10.3 %psum.22 = f32[64,64]{0,1:T(8,128)S(1)} all-reduce(f32[64,64]{0,1:T(8,128)S(1)} %fusion.8), channel_id=1, replica_groups=mesh['dp'=8,'mp'=4] {'mp'}, use_global_device_ids=true, to_apply=%region_1.0 | all-reduce | flops 4096 | bytes 32768 | tf_op jit(solution)/shard_map/psum | solution.py:35
  185.1 0.1 copy.12
  185.2 5.8 %cholesky.16 = f32[64,64]{1,0:T(8,128)S(1)} custom-call(f32[64,64]{1,0:T(8,128)S(1)} %fusion.5), custom_call_target="Cholesky" | custom-call | tf_op jit(solution)/shard_map/jit(cholesky)/cholesky | solution.py:36
  191.1 0.6 compare_reduce_fusion
  191.8 0.7 fusion.3
  192.4 4.9 %custom-call.7 = f32[1,64,64]{1,2,0:T(8,128)S(1)} custom-call(f32[1,64,64]{2,1,0:T(8,128)S(1)} %fusion.3), custom_call_target="InvertDiagBlocksLowerTriangular" | custom-call | tf_op jit(solution)/shard_map/jit(_solve_triangular)/triangular_solve | solution.py:37
  197.3 1.3 convolution_convert_fusion
  198.6 5.4 %fusion.9 = f32[6144,64]{0,1:T(8,128)S(1)} fusion(bf16[768,64]{0,1:T(8,128)(2,1)S(1)} %convolution_convert_fusion, bf16[768,6144]{1,0:T(8,128)(2,1)} %copy-done.1), kind=kOutput, calls=%fused_computation.19 | convolution fusion | flops 603979776 | bytes 11108352 | tf_op jit(solution)/shard_map/dot_general | solution.py:41
  204.1 55.9 %all-reduce.4 = bf16[6144,64]{0,1:T(8,128)(2,1)S(1)} all-reduce(f32[6144,64]{0,1:T(8,128)S(1)} %fusion.9), channel_id=1, replica_groups=mesh['dp'=8,'mp'=4] {'dp','mp'}, use_global_device_ids=true, to_apply=%region_4.5 | all-reduce | flops 393216 | bytes 2359296 | tf_op jit(solution)/shard_map/psum | solution.py:44
  259.9 0.0 copy-start.2
  260.0 0.0 copy-start.3
  260.0 7.8 %fusion.1 = bf16[1,768,6144]{2,1,0:T(8,128)(2,1)} fusion(bf16[768,64]{0,1:T(8,128)(2,1)S(1)} %convolution_convert_fusion, bf16[6144,64]{0,1:T(8,128)(2,1)S(1)} %all-reduce.4, bf16[768,6144]{1,0:T(8,128)(2,1)} %copy-done.1), kind=kOutput, calls=%fused_computation.3 | convolution fusion | flops 622854144 | bytes 19759104 | tf_op jit(solution)/shard_map/dot_general | solution.py:50
  267.8 0.0 copy-done.2
  267.8 0.0 copy-done.3
  267.8 1.9 multiply_add_fusion
  (2 shorter events, 0.0 us)
Async XLA Ops:
  7.2 77.3 %copy-start = (bf16[512,768]{1,0:T(8,128)(2,1)S(1)}, bf16[512,768]{1,0:T(8,128)(2,1)}, u32[]{:S(2)}) copy-start(bf16[512,768]{1,0:T(8,128)(2,1)} %param.5) | copy-start | bytes 2359300
  7.2 166.4 %all-reduce.3.cloned.1.call-start = ((), (), s32[]{:S(2)}) async-start(), calls=%async_computation.1 | async-start | bytes 393216 | tf_op jit(solution)/shard_map/psum | solution.py:28
  84.4 13.6 %copy-start.4 = (bf16[6144,64]{0,1:T(8,128)(2,1)S(1)}, bf16[6144,64]{0,1:T(8,128)(2,1)}, u32[]{:S(2)}) copy-start(bf16[6144,64]{0,1:T(8,128)(2,1)} %param.8) | copy-start | bytes 2359300
  94.3 3.7 %copy-start.1 = (bf16[768,6144]{1,0:T(8,128)(2,1)}, bf16[768,6144]{1,0:T(8,128)(2,1)S(1)}, u32[]{:S(2)}) copy-start(bf16[768,6144]{1,0:T(8,128)(2,1)S(1)} %fusion) | copy-start | bytes 28311556
  259.9 7.8 %copy-start.2 = (bf16[6144,64]{0,1:T(8,128)(2,1)}, bf16[6144,64]{0,1:T(8,128)(2,1)S(1)}, u32[]{:S(2)}) copy-start(bf16[6144,64]{0,1:T(8,128)(2,1)S(1)} %all-reduce.4) | copy-start | bytes 2359300
  260.0 7.8 %copy-start.3 = (f32[768,768]{1,0:T(8,128)S(1)}, f32[768,768]{1,0:T(8,128)}, u32[]{:S(2)}) copy-start(f32[768,768]{1,0:T(8,128)} %param.9) | copy-start | bytes 7077892
Sparse Core Ops, SparseCore 0:
  101.8 71.6 all-reduce.2
